TPU v7x, 512 devices: a whole 4x4x16 slice. The times are simulated.
512 devices in a mesh: slab: 16 (over z_lo, core), src: 32 (over y, x, z_hi).
Axes of the slice: x: 4, y: 4, z: 16 (z_hi: 2, z_lo: 8; z = z_hi * 8 + z_lo), core: 2. Of those that a mesh axis runs over, the one named last changes fastest.
Arguments:
- trace_values: bfloat16 [32, 8192, 128], P('src', 'slab'), may hold values from -6 to 6
- trace_owner: int32 [32, 8192, 1], P('src', 'slab'), may hold values from 0 to 15; in each aligned block of 512 rows (0 to 511, 512 to 1023, ..., all dimensions but the last counted through in order) at most 64 rows name the same one
- trace_source: int32 [32, 8192], P('src', 'slab'), may hold values from 0 to 511
- source_fields: bfloat16 [2, 8192, 16384], P(None, 'slab', 'src'), may hold values from -0.03125 to 0.03125
- green_fields: bfloat16 [2, 2048, 16384], P(None, 'slab', 'src'), may hold values from -0.0625 to 0.0625
Outputs:
- gradient: float32 [16384], P('src')
Inputs may be any that keep to these rules, and one draw needn't show every extreme that they name: `trace_owner`: among the traces of one device, no owner is named by more than 64 traces, a bound that some block reaches.
All inputs are finite; a program needn't handle non-finite values.
Results may differ from a plain program's by a relative error of at most 0.0026.
Values may be sent and summed in bfloat16 or wider, within the bound.
A program may use at most 64 MiB of HBM per device.

v0:
```python
import jax
import jax.numpy as jnp
from jax import lax
from jax.sharding import PartitionSpec as P


def on_device(trace_values, trace_owner, trace_source, source_fields, green_fields):
    values = trace_values[0]
    owners = trace_owner[0, :, 0]
    locals_id = trace_source[0]
    trace_count = values.shape[0]
    width = values.shape[1]
    half_width = width // 2
    slab_count = lax.axis_size("slab")
    src_count = lax.axis_size("src")
    sources_here = source_fields.shape[1]
    source_ids = jnp.arange(sources_here, dtype=jnp.int32)
    iota_high = (source_ids // 32).astype(jnp.bfloat16)
    iota_low = (source_ids % 32).astype(jnp.bfloat16)
    capacity = 2 * trace_count // slab_count
    owner_hits = (owners[:, None] == jnp.arange(slab_count, dtype=jnp.int32)[None, :]).astype(
        jnp.int32
    )
    ranks = jnp.sum(jnp.cumsum(owner_hits, axis=0) * owner_hits, axis=1) - 1
    slots = owners * capacity + ranks
    placing = (
        jnp.arange(slab_count * capacity, dtype=jnp.int32)[:, None] == slots[None, :]
    ).astype(jnp.bfloat16)
    sent_values = jnp.dot(placing, values, preferred_element_type=jnp.float32).astype(jnp.bfloat16)
    labels = jnp.stack([locals_id // 32 + 1, locals_id % 32 + 1], axis=1).astype(jnp.bfloat16)
    sent_labels = (jnp.dot(placing, labels, preferred_element_type=jnp.float32) - 1.0).astype(
        jnp.bfloat16
    )
    got_values, got_labels = (
        lax.all_to_all(
            sent_values.reshape(slab_count, capacity, width),
            "slab",
            split_axis=0,
            concat_axis=0,
            tiled=True,
        ),
        lax.all_to_all(
            sent_labels.reshape(slab_count, capacity, 2),
            "slab",
            split_axis=0,
            concat_axis=0,
            tiled=True,
        ),
    )
    flat_labels = got_labels.reshape(-1, 2)
    picks = (
        (iota_high[:, None] == flat_labels[None, :, 0])
        & (iota_low[:, None] == flat_labels[None, :, 1])
    ).astype(jnp.bfloat16)
    assembled = jnp.dot(picks, got_values.reshape(-1, width), preferred_element_type=jnp.float32)
    residual_piece = assembled.astype(jnp.bfloat16)
    residual_rows = lax.all_gather(residual_piece, "src", axis=1, tiled=True)
    split_rows = residual_rows.reshape(sources_here, src_count, 2, half_width)
    res_real = split_rows[:, :, 0, :].reshape(sources_here, src_count * half_width)
    res_imag = split_rows[:, :, 1, :].reshape(sources_here, src_count * half_width)
    piece = lax.all_gather(green_fields, "slab", axis=1, tiled=True)
    adj_real = jnp.dot(res_real, piece[0], preferred_element_type=jnp.float32) + jnp.dot(
        res_imag, piece[1], preferred_element_type=jnp.float32
    )
    adj_imag = jnp.dot(res_real, piece[1], preferred_element_type=jnp.float32) - jnp.dot(
        res_imag, piece[0], preferred_element_type=jnp.float32
    )
    adj_real, adj_imag = (adj_real, adj_imag)
    partial_value = jnp.sum(
        source_fields[0].astype(jnp.float32) * adj_real
        - source_fields[1].astype(jnp.float32) * adj_imag,
        axis=0,
    )
    return lax.psum(partial_value, "slab")


def solution(mesh):
    in_specs = (
        P("src", "slab", None),
        P("src", "slab", None),
        P("src", "slab"),
        P(None, "slab", "src"),
        P(None, "slab", "src"),
    )
    out_specs = P("src")
    return jax.shard_map(
        on_device, mesh=mesh, in_specs=in_specs, out_specs=out_specs, check_vma=False
    )
```

profile of v0, /device:TPU:6, one launch (start us, length us, event | category | flops | bytes accessed | tf_op | source)
XLA Modules:
  0.0 432.0 jit_solution(941762704033851159)
XLA Ops:
  6.5 0.0 copy-start
  6.5 0.7 fusion.31
  7.3 1.1 reduce-window.6
  8.4 0.2 slice_reduce_fusion
  8.7 0.8 fusion.30
  9.4 0.7 add_add_fusion
  10.1 0.7 add_convert_fusion
  10.8 0.5 fusion.21
  11.3 0.1 reshape.180
  11.4 0.6 copy.12
  12.0 12.6 %all-to-all-start = ((bf16[16,64,2]{1,2,0:T(2,128)(2,1)}), bf16[16,64,2]{1,2,0:T(2,128)(2,1)S(1)}, u32[]{:S(2)}, u32[]{:S(2)}) async-start(bf16[16,64,2]{1,2,0:T(2,128)(2,1)} %copy.12), calls=%async_computation | async-start | bytes 16384 | tf_op jit(solution)/shard_map/all_to_all | solution.py:42
  24.6 0.0 copy-done
  24.6 1.2 fusion.16
  25.8 9.2 %all-to-all-done = bf16[16,64,2]{1,2,0:T(2,128)(2,1)S(1)} async-done(((bf16[16,64,2]{1,2,0:T(2,128)(2,1)}), bf16[16,64,2]{1,2,0:T(2,128)(2,1)S(1)}, u32[]{:S(2)}, u32[]{:S(2)}) %all-to-all-start) | async-done | bytes 4128 | tf_op jit(solution)/shard_map/all_to_all | solution.py:42
  35.0 3.5 all-to-all-start.1
  38.5 0.0 all-gather.3.cloned.1.call-start
  38.6 0.1 reshape.181
  38.7 14.7 %all-to-all-done.1 = bf16[16,64,128]{2,1,0:T(8,128)(2,1)S(1)} async-done(((bf16[16,64,128]{2,1,0:T(8,128)(2,1)}), bf16[16,64,128]{2,1,0:T(8,128)(2,1)S(1)}, u32[]{:S(2)}, u32[]{:S(2)}) %all-to-all-start.1) | async-done | bytes 262176 | tf_op jit(solution)/shard_map/all_to_all | solution.py:35
  53.4 1.3 fusion.17
  54.7 0.0 all-gather.3.cloned.1.call-update
  54.7 0.0 all-gather.5.cloned.1.call-start
  54.8 0.7 all-gather.5.cloned.1.call-update
  55.5 208.7 %all-gather.3.cloned.1.call-done = bf16[512,4096]{1,0:T(8,128)(2,1)} async-done(((bf16[512,128]{1,0:T(8,128)(2,1)}), bf16[512,4096]{1,0:T(8,128)(2,1)}) %all-gather.3.cloned.1.call-update) | async-done | bytes 4194320 | tf_op jit(solution)/shard_map/all_gather | solution.py:57
  264.2 6.5 %copy.14 = bf16[512,4096]{0,1:T(8,128)(2,1)} copy(bf16[512,4096]{1,0:T(8,128)(2,1)} %all-gather.3.cloned.1.call-done) | data formatting | bytes 8388608 | tf_op jit(solution)/shard_map/all_gather | solution.py:57
  270.7 4.0 fusion.47
  274.7 89.8 %all-gather.5.cloned.1.call-done = bf16[2,2048,512]{2,1,0:T(8,128)(2,1)} async-done(((bf16[2,128,512]{2,1,0:T(8,128)(2,1)}), bf16[2,2048,512]{2,1,0:T(8,128)(2,1)}) %all-gather.5.cloned.1.call-update) | async-done | bytes 4194320 | tf_op jit(solution)/shard_map/all_gather | solution.py:61
  364.5 0.0 copy-start.1
  364.5 3.0 fusion.7
  367.5 0.0 copy-done.1
  367.5 0.0 copy-start.2
  367.5 0.0 copy-start.3
  367.5 3.0 fusion.6
  370.6 0.0 copy-done.2
  370.6 0.1 copy-done.3
  370.6 1.3 fusion.11
  371.9 1.3 fusion.15
  373.2 51.9 %psum.7 = f32[512]{0:T(512)} all-reduce(f32[512]{0:T(512)S(1)} %fusion.15), channel_id=1, replica_groups=mesh['slab'=16,'src'=32] {'slab'}, use_global_device_ids=true, to_apply=%region_4.5 | all-reduce | flops 512 | bytes 4096 | tf_op jit(solution)/shard_map/psum | solution.py:74
  (6 shorter events, 0.1 us)
Async XLA Ops:
  6.5 18.1 %copy-start = (bf16[1,512,128]{2,1,0:T(8,128)(2,1)S(1)}, bf16[1,512,128]{2,1,0:T(8,128)(2,1)}, u32[]{:S(2)}) copy-start(bf16[1,512,128]{2,1,0:T(8,128)(2,1)} %param.5) | copy-start | bytes 393220
  12.0 23.0 %all-to-all-start = ((bf16[16,64,2]{1,2,0:T(2,128)(2,1)}), bf16[16,64,2]{1,2,0:T(2,128)(2,1)S(1)}, u32[]{:S(2)}, u32[]{:S(2)}) async-start(bf16[16,64,2]{1,2,0:T(2,128)(2,1)} %copy.12), calls=%async_computation | async-start | bytes 16384 | tf_op jit(solution)/shard_map/all_to_all | solution.py:42
  35.0 18.5 %all-to-all-start.1 = ((bf16[16,64,128]{2,1,0:T(8,128)(2,1)}), bf16[16,64,128]{2,1,0:T(8,128)(2,1)S(1)}, u32[]{:S(2)}, u32[]{:S(2)}) async-start(bf16[16,64,128]{2,1,0:T(8,128)(2,1)} %bitcast.6), calls=%async_computation.1 | async-start | bytes 524288 | tf_op jit(solution)/shard_map/all_to_all | solution.py:35
  38.5 225.7 %all-gather.3.cloned.1.call-start = ((), (), s32[]{:S(2)}) async-start(), calls=%async_computation.2 | async-start | bytes 4325376 | tf_op jit(solution)/shard_map/all_gather | solution.py:57
  54.7 309.8 %all-gather.5.cloned.1.call-start = ((), (), s32[]{:S(2)}) async-start(), calls=%async_computation.3 | async-start | bytes 4456448 | tf_op jit(solution)/shard_map/all_gather | solution.py:61
  364.5 3.0 copy-start.1
  367.5 3.0 copy-start.2
  367.5 3.1 copy-start.3
Sparse Core Ops, SparseCore 0:
  54.8 209.3 all-gather.2
  266.3 98.1 all-gather.4
where the time goes:
time: 432 us
  waiting for transfers between devices  323 us (75%)
  blocking collectives  51.9 us (12%)
  starting transfers between devices  16.2 us (4%)
  between operations  13.5 us (3%)
  local copies, waits for them, and re-layouts  11.6 us (3%)
  matrix products  11.5 us (3%)
    all_gather x1, waiting for transfers between devices, on_device(): residual_rows = lax.all_gather(residual_piece, 'src', axis=1, tiled=True)  209 us
    all_gather x1, waiting for transfers between devices, on_device(): piece = lax.all_gather(green_fields, 'slab', axis=1, tiled=True)  89.8 us
    psum x1, blocking collectives, on_device(): return lax.psum(partial_value, 'slab')  51.9 us
    all_to_all x1, waiting for transfers between devices, on_device(): lax.all_to_all(sent_values.reshape(slab_count, capacity, width), 'slab',...  14.7 us
    all_to_all x1, starting transfers between devices, on_device(): lax.all_to_all(sent_labels.reshape(slab_count, capacity, 2), 'slab', spli...  12.6 us
    all_to_all x1, waiting for transfers between devices, on_device(): lax.all_to_all(sent_labels.reshape(slab_count, capacity, 2), 'slab', spli...  9.19 us
  transfers between devices with their start and end apart: 4, of which 4 were waited for; matrix products, arithmetic and copies ran while one was open for 3% of the time, Pallas kernels for 0%

commit v1 on v0

--- a/solution.py
+++ b/solution.py
@@ -54,7 +54,7 @@
     ).astype(jnp.bfloat16)
     assembled = jnp.dot(picks, got_values.reshape(-1, width), preferred_element_type=jnp.float32)
     residual_piece = assembled.astype(jnp.bfloat16)
-    residual_rows = lax.all_gather(residual_piece, "src", axis=1, tiled=True)
+    residual_rows = jnp.concatenate(lax.all_gather(residual_piece, "src"), axis=1)
     split_rows = residual_rows.reshape(sources_here, src_count, 2, half_width)
     res_real = split_rows[:, :, 0, :].reshape(sources_here, src_count * half_width)
     res_imag = split_rows[:, :, 1, :].reshape(sources_here, src_count * half_width)

time: 432 us -> 391 us (0.905)
  waiting for transfers between devices: 323 us -> 282 us
    all_gather x1, waiting for transfers between devices: 209 us -> 160 us  [on_device(): lax.all_gather(residual_piece, 'src')]
    all_gather x1, waiting for transfers between devices: 89.8 us -> 97.1 us  [on_device(): piece = lax.all_gather(green_fields, 'slab', axis=1, tiled=True)]
where the time goes in v1:
time: 391 us
  waiting for transfers between devices  282 us (72%)
  blocking collectives  51.9 us (13%)
  starting transfers between devices  16.2 us (4%)
  between operations  13.5 us (3%)
  local copies, waits for them, and re-layouts  11.6 us (3%)
  matrix products  11.5 us (3%)
  other arithmetic  4.07 us (1%)
    all_gather x1, waiting for transfers between devices, on_device(): lax.all_gather(residual_piece, 'src')  160 us
    all_gather x1, waiting for transfers between devices, on_device(): piece = lax.all_gather(green_fields, 'slab', axis=1, tiled=True)  97.1 us
    psum x1, blocking collectives, on_device(): return lax.psum(partial_value, 'slab')  51.9 us
    all_to_all x1, waiting for transfers between devices, on_device(): lax.all_to_all(sent_values.reshape(slab_count, capacity, width), 'slab',...  14.7 us
    all_to_all x1, starting transfers between devices, on_device(): lax.all_to_all(sent_labels.reshape(slab_count, capacity, 2), 'slab', spli...  12.6 us
    all_to_all x1, waiting for transfers between devices, on_device(): lax.all_to_all(sent_labels.reshape(slab_count, capacity, 2), 'slab', spli...  9.19 us
  transfers between devices with their start and end apart: 4, of which 4 were waited for; matrix products, arithmetic and copies ran while one was open for 3% of the time, Pallas kernels for 0%

profile of v1, /device:TPU:6, one launch (start us, length us, event | category | flops | bytes accessed | tf_op | source)
XLA Modules:
  0.0 391.0 jit_solution(7246964289313251789)
XLA Ops:
  6.5 0.0 copy-start
  6.5 0.7 fusion.31
  7.3 1.1 reduce-window.6
  8.4 0.2 slice_reduce_fusion
  8.7 0.8 fusion.30
  9.4 0.7 add_add_fusion
  10.1 0.7 add_convert_fusion
  10.8 0.5 fusion.21
  11.3 0.1 reshape.180
  11.4 0.6 copy.12
  12.0 12.6 %all-to-all-start = ((bf16[16,64,2]{1,2,0:T(2,128)(2,1)}), bf16[16,64,2]{1,2,0:T(2,128)(2,1)S(1)}, u32[]{:S(2)}, u32[]{:S(2)}) async-start(bf16[16,64,2]{1,2,0:T(2,128)(2,1)} %copy.12), calls=%async_computation | async-start | bytes 16384 | tf_op jit(solution)/shard_map/all_to_all | solution.py:42
  24.6 0.0 copy-done
  24.6 1.2 fusion.16
  25.8 9.2 %all-to-all-done = bf16[16,64,2]{1,2,0:T(2,128)(2,1)S(1)} async-done(((bf16[16,64,2]{1,2,0:T(2,128)(2,1)}), bf16[16,64,2]{1,2,0:T(2,128)(2,1)S(1)}, u32[]{:S(2)}, u32[]{:S(2)}) %all-to-all-start) | async-done | bytes 4128 | tf_op jit(solution)/shard_map/all_to_all | solution.py:42
  35.0 3.5 all-to-all-start.1
  38.5 0.0 all-gather.6.cloned.1.call-start
  38.6 0.1 reshape.181
  38.7 14.7 %all-to-all-done.1 = bf16[16,64,128]{2,1,0:T(8,128)(2,1)S(1)} async-done(((bf16[16,64,128]{2,1,0:T(8,128)(2,1)}), bf16[16,64,128]{2,1,0:T(8,128)(2,1)S(1)}, u32[]{:S(2)}, u32[]{:S(2)}) %all-to-all-start.1) | async-done | bytes 262176 | tf_op jit(solution)/shard_map/all_to_all | solution.py:35
  53.4 1.3 fusion.17
  54.7 0.0 all-gather.6.cloned.1.call-update
  54.7 0.0 all-gather.4.cloned.1.call-start
  54.8 0.7 all-gather.4.cloned.1.call-update
  55.5 160.5 %all-gather.6.cloned.1.call-done = bf16[16384,128]{1,0:T(8,128)(2,1)} async-done(((bf16[512,128]{1,0:T(8,128)(2,1)}), bf16[16384,128]{1,0:T(8,128)(2,1)}) %all-gather.6.cloned.1.call-update) | async-done | bytes 4194320 | tf_op jit(solution)/shard_map/all_gather | solution.py:57
  215.9 6.5 %copy.14 = bf16[32,512,128]{1,2,0:T(8,128)(2,1)} copy(bf16[32,512,128]{2,1,0:T(8,128)(2,1)} %bitcast.82) | data formatting | bytes 8388608 | tf_op jit(solution)/shard_map/all_gather | solution.py:57
  222.5 4.0 %fusion.47 = (bf16[512,32,1,64]{0,3,2,1:T(8,128)(2,1)}, bf16[512,32,1,64]{0,3,2,1:T(8,128)(2,1)S(1)}) fusion(bf16[512,32,2,64]{0,3,2,1:T(8,128)(2,1)} %bitcast.81), kind=kLoop, calls=%fused_computation.67 | loop fusion | bytes 8388608 | tf_op jit(solution)/shard_map/slice | solution.py:60
  226.4 97.1 %all-gather.4.cloned.1.call-done = bf16[2,2048,512]{2,1,0:T(8,128)(2,1)} async-done(((bf16[2,128,512]{2,1,0:T(8,128)(2,1)}), bf16[2,2048,512]{2,1,0:T(8,128)(2,1)}) %all-gather.4.cloned.1.call-update) | async-done | bytes 4194320 | tf_op jit(solution)/shard_map/all_gather | solution.py:61
  323.5 0.0 copy-start.1
  323.5 3.0 fusion.7
  326.5 0.0 copy-done.1
  326.5 0.0 copy-start.2
  326.5 0.0 copy-start.3
  326.5 3.0 fusion.6
  329.6 0.0 copy-done.2
  329.6 0.1 copy-done.3
  329.6 1.3 fusion.11
  330.9 1.3 fusion.15
  332.2 51.9 %psum.7 = f32[512]{0:T(512)} all-reduce(f32[512]{0:T(512)S(1)} %fusion.15), channel_id=1, replica_groups=mesh['slab'=16,'src'=32] {'slab'}, use_global_device_ids=true, to_apply=%region_4.5 | all-reduce | flops 512 | bytes 4096 | tf_op jit(solution)/shard_map/psum | solution.py:74
  (6 shorter events, 0.1 us)
Async XLA Ops:
  6.5 18.1 %copy-start = (bf16[1,512,128]{2,1,0:T(8,128)(2,1)S(1)}, bf16[1,512,128]{2,1,0:T(8,128)(2,1)}, u32[]{:S(2)}) copy-start(bf16[1,512,128]{2,1,0:T(8,128)(2,1)} %param.5) | copy-start | bytes 393220
  12.0 23.0 %all-to-all-start = ((bf16[16,64,2]{1,2,0:T(2,128)(2,1)}), bf16[16,64,2]{1,2,0:T(2,128)(2,1)S(1)}, u32[]{:S(2)}, u32[]{:S(2)}) async-start(bf16[16,64,2]{1,2,0:T(2,128)(2,1)} %copy.12), calls=%async_computation | async-start | bytes 16384 | tf_op jit(solution)/shard_map/all_to_all | solution.py:42
  35.0 18.5 %all-to-all-start.1 = ((bf16[16,64,128]{2,1,0:T(8,128)(2,1)}), bf16[16,64,128]{2,1,0:T(8,128)(2,1)S(1)}, u32[]{:S(2)}, u32[]{:S(2)}) async-start(bf16[16,64,128]{2,1,0:T(8,128)(2,1)} %bitcast.6), calls=%async_computation.1 | async-start | bytes 524288 | tf_op jit(solution)/shard_map/all_to_all | solution.py:35
  38.5 177.4 %all-gather.6.cloned.1.call-start = ((), (), s32[]{:S(2)}) async-start(), calls=%async_computation.3 | async-start | bytes 4325376 | tf_op jit(solution)/shard_map/all_gather | solution.py:57
  54.7 268.8 %all-gather.4.cloned.1.call-start = ((), (), s32[]{:S(2)}) async-start(), calls=%async_computation.2 | async-start | bytes 4456448 | tf_op jit(solution)/shard_map/all_gather | solution.py:61
  323.5 3.0 copy-start.1
  326.5 3.1 copy-start.2
  326.5 3.1 copy-start.3
Sparse Core Ops, SparseCore 0:
  54.8 161.0 all-gather.5
  218.0 105.4 all-gather.3
